TPU v7x, 32 devices: a whole 2x2x4 slice. The times are simulated.
32 devices in a mesh: outer: 8 (over z, y), inner: 4 (over x, core).
Axes of the slice: x: 2, y: 2, z: 4, core: 2. Of those that a mesh axis runs over, the one named last changes fastest.
Arguments:
- hidden: bfloat16 [4096, 1024], P(('outer', 'inner')), may hold values from -6 to 6
- x_act: bfloat16 [4096, 2048], P(('outer', 'inner')), may hold values from -6 to 6
- dt_step: float32 [4096, 32], P(('outer', 'inner')), may hold values from 0.00421875 to 0.44, as said below
- log_decay: float32 [4096, 32], P(('outer', 'inner')), may hold values from -0.81 to -7.080078e-06, as said below
- w_bc: bfloat16 [1024, 128], P(('outer', 'inner')), may hold values from -0.1875 to 0.1875
- grad_y: bfloat16 [4096, 2048], P(('outer', 'inner')), may hold values from -0.19921875 to 0.19921875
Outputs:
- grad_x: float32 [4096, 2048], P(('outer', 'inner'))
- grad_hidden: float32 [4096, 1024], P(('outer', 'inner'))
- grad_proj: float32 [1024, 128], P(('outer', 'inner'))
Inputs may be any that keep to these rules, and one draw needn't show every extreme that they name: `dt_step`: Positive; constant in scale within each head apart from a factor within e**-0.5 to e**0.5. `log_decay`: Negative.
All inputs are finite; a program needn't handle non-finite values.
Results may differ from a plain program's by a relative error of at most 0.0029.
Values may be sent and summed in bfloat16 or wider, within the bound.
No kernel may reach another device: no remote copies, remote signals or barrier semaphores. Data moves between devices by JAX's collectives and lax.ppermute only.
A program may use at most 64 MiB of HBM per device.

v0:
```python
import math
import jax
import jax.numpy as jnp
from jax import lax
from jax.sharding import PartitionSpec as P

BLOCK = 128
HIGH = lax.Precision.HIGHEST


def carried_in(array, axis, combine, identity, reverse):
    count, mine = (lax.axis_size(axis), lax.axis_index(axis))
    everything = jax.tree.map(lambda part: lax.all_gather(part, axis), array)
    start = jax.tree.map(
        lambda part, zero: jnp.broadcast_to(jnp.asarray(zero, part.dtype), part.shape),
        array,
        identity,
    )

    def step(k, before):
        at = count - 1 - k if reverse else k
        reached = at > mine if reverse else at < mine
        new = combine(before, jax.tree.map(lambda part: part[at], everything))
        return jax.tree.map(lambda a, b: jnp.where(reached, a, b), new, before)

    return lax.fori_loop(0, count, step, start)


def block_step(carried, pieces):
    inputs, decays, b_rows, c_rows = pieces
    length = inputs.shape[0]
    running = jnp.cumsum(decays, axis=0)
    row_ids = lax.broadcasted_iota(jnp.int32, (length, length), 0)
    col_ids = lax.broadcasted_iota(jnp.int32, (length, length), 1)
    causal = row_ids >= col_ids
    spread = running.T[:, :, None] - running.T[:, None, :]
    segment = jnp.where(causal[None], jnp.exp(jnp.where(causal[None], spread, 0.0)), 0.0)
    scores = jnp.einsum("in,jn->ij", c_rows, b_rows, precision=HIGH)
    outputs = jnp.einsum("hij,jhp->ihp", segment * scores[None], inputs, precision=HIGH)
    outputs = outputs + jnp.exp(running)[:, :, None] * jnp.einsum(
        "in,hpn->ihp", c_rows, carried, precision=HIGH
    )
    final_sum = running[-1]
    weights = jnp.exp(final_sum[None, :] - running)
    updated = jnp.exp(final_sum)[:, None, None] * carried + jnp.einsum(
        "jhp,jn->hpn", inputs * weights[:, :, None], b_rows, precision=HIGH
    )
    return (updated, outputs)


def scan_block(inputs, decays, b_rows, c_rows, carried, length):
    count = inputs.shape[0] // length
    pieces = (
        inputs.reshape((count, length) + inputs.shape[1:]),
        decays.reshape((count, length, decays.shape[1])),
        b_rows.reshape((count, length, b_rows.shape[1])),
        c_rows.reshape((count, length, c_rows.shape[1])),
    )
    final_state, outputs = lax.scan(block_step, carried, pieces)
    return (outputs.reshape(inputs.shape), final_state)


def slice_combine(earlier, later):
    return (earlier[0] + later[0], jnp.exp(later[0])[:, None] * earlier[1] + later[1])


def slice_step(carry, item):
    return (slice_combine(carry, item), carry)


def per_device(hidden, x_act, dt_step, log_decay, w_bc, grad_y):
    weights_full = lax.all_gather(w_bc, ("outer", "inner"), axis=0, tiled=True)
    state_width = weights_full.shape[1] // 2
    row_count = hidden.shape[0]
    head_count = dt_step.shape[1]
    head_size = x_act.shape[1] // head_count
    projected = jnp.dot(hidden, weights_full, preferred_element_type=jnp.float32)
    b_rows = projected[:, :state_width]
    c_rows = projected[:, state_width:]
    inputs = dt_step[:, :, None] * x_act.astype(jnp.float32).reshape(
        row_count, head_count, head_size
    )
    cotangent = grad_y.astype(jnp.float32).reshape(row_count, head_count, head_size)
    running = jnp.cumsum(log_decay, axis=0)
    totals = running[-1]
    own_state = jnp.einsum(
        "jhp,jn->hpn",
        inputs * jnp.exp(totals[None, :] - running)[:, :, None],
        b_rows,
        precision=HIGH,
    )
    own_adjoint = jnp.einsum(
        "ihp,in->hpn", cotangent * jnp.exp(running)[:, :, None], c_rows, precision=HIGH
    )
    inner_count = lax.axis_size("inner")
    flat_width = head_size * state_width
    paired = jnp.stack(
        [own_state.reshape(head_count, flat_width), own_adjoint.reshape(head_count, flat_width)]
    )[None]
    totals_wide = jnp.broadcast_to(totals[None, None, :, None], (1, 1, head_count, inner_count))
    slices, all_totals = (
        lax.all_to_all(paired, "inner", split_axis=3, concat_axis=0, tiled=True),
        lax.all_to_all(totals_wide, "inner", split_axis=3, concat_axis=0, tiled=True),
    )
    all_totals = all_totals[:, 0, :, 0]
    zero_slice = (jnp.zeros((head_count,), jnp.float32), jnp.zeros_like(slices[0, 0]))
    forward_total, forward_prior = lax.scan(slice_step, zero_slice, (all_totals, slices[:, 0]))
    backward_total, backward_after = lax.scan(
        slice_step, zero_slice, (all_totals, slices[:, 1]), reverse=True
    )
    coarse_forward = carried_in(forward_total, "outer", slice_combine, zero_slice, False)
    coarse_backward = carried_in(backward_total, "outer", slice_combine, zero_slice, True)
    state_part = jnp.exp(forward_prior[0])[:, :, None] * coarse_forward[1][None] + forward_prior[1]
    adjoint_part = (
        jnp.exp(backward_after[0])[:, :, None] * coarse_backward[1][None] + backward_after[1]
    )
    returned = lax.all_to_all(
        jnp.stack([state_part, adjoint_part], 1), "inner", split_axis=0, concat_axis=3, tiled=True
    )
    state_in = returned[0, 0].reshape(head_count, head_size, state_width)
    adjoint_out = returned[0, 1].reshape(head_count, head_size, state_width)

    def forward(inputs, b_rows, c_rows):
        return scan_block(inputs, log_decay, b_rows, c_rows, state_in, BLOCK)

    outputs, pullback = jax.vjp(forward, inputs, b_rows, c_rows)
    d_in, d_b, d_c = pullback((cotangent, adjoint_out))
    grad_x = (dt_step[:, :, None] * d_in).reshape(row_count, head_count * head_size)
    d_proj = jnp.concatenate([d_b, d_c], axis=1)
    d_low = d_proj.astype(jnp.bfloat16)
    grad_hidden = lax.dot_general(
        d_low, weights_full, (((1,), (1,)), ((), ())), preferred_element_type=jnp.float32
    )
    scale = 1.0 / math.sqrt(row_count * lax.axis_size("outer") * lax.axis_size("inner"))
    grad_proj = lax.psum_scatter(
        lax.dot_general(hidden, d_low, (((0,), (0,)), ((), ())), preferred_element_type=jnp.float32)
        * scale,
        ("outer", "inner"),
        scatter_dimension=0,
        tiled=True,
    )
    return (grad_x, grad_hidden, grad_proj)


def solution(mesh):
    in_specs = (
        P(("outer", "inner"), None),
        P(("outer", "inner"), None),
        P(("outer", "inner"), None),
        P(("outer", "inner"), None),
        P(("outer", "inner"), None),
        P(("outer", "inner"), None),
    )
    out_specs = (
        P(("outer", "inner"), None),
        P(("outer", "inner"), None),
        P(("outer", "inner"), None),
    )
    return jax.shard_map(
        per_device, mesh=mesh, in_specs=in_specs, out_specs=out_specs, check_vma=False
    )
```

profile of v0, /device:TPU:0, one launch (start us, length us, event | category | flops | bytes accessed | tf_op | source)
XLA Modules:
  0.0 382.8 jit_solution(757989280330233703)
XLA Ops:
  7.2 0.9 copy.63
  8.3 44.2 %all_gather.27 = bf16[1024,128]{1,0:T(8,128)(2,1)S(1)} all-gather(bf16[32,128]{1,0:T(8,128)(2,1)} %param.18), channel_id=1, replica_groups=mesh['outer'=8,'inner'=4] {'outer','inner'}, dimensions={0}, use_global_device_ids=true | all-gather | bytes 270336 | tf_op jit(solution)/shard_map/all_gather | solution.py:72
  52.5 1.4 copy.64
  54.3 1.0 fusion.29
  56.3 1.0 fusion.27
  57.7 4.4 %copy.68 = f32[2,32,4096]{1,0,2:T(2,128)} copy(f32[2,32,4096]{2,1,0:T(8,128)S(1)} %pad_maximum_fusion) | data formatting | bytes 2097152 | tf_op jit(solution)/shard_map/stack | solution.py:97
  62.1 4.7 %bitcast_bitcast_fusion = f32[4096,1,2,32]{3,2,1,0:T(2,128)} fusion(f32[2,32,4096]{1,0,2:T(2,128)} %copy.68), kind=kLoop, calls=%fused_computation.87 | loop fusion | bytes 2097152
  66.8 6.5 %reshape.273 = f32[4,1,65536]{2,1,0:T(1,128)} reshape(f32[4096,1,2,32]{3,2,1,0:T(2,128)} %bitcast_bitcast_fusion) | data formatting | bytes 2097152
  73.3 4.4 %all-to-all-start.1 = ((f32[4,1,65536]{2,1,0:T(1,128)}), f32[4,1,65536]{2,1,0:T(1,128)}, u32[]{:S(2)}, u32[]{:S(2)}) async-start(f32[4,1,65536]{2,1,0:T(1,128)} %reshape.273), calls=%async_computation.1 | async-start | bytes 2097152 | tf_op jit(solution)/shard_map/all_to_all | solution.py:102
  78.9 13.3 %all-to-all-done.1 = f32[4,1,65536]{2,1,0:T(1,128)} async-done(((f32[4,1,65536]{2,1,0:T(1,128)}), f32[4,1,65536]{2,1,0:T(1,128)}, u32[]{:S(2)}, u32[]{:S(2)}) %all-to-all-start.1) | async-done | bytes 1048608 | tf_op jit(solution)/shard_map/all_to_all | solution.py:102
  92.8 3.8 all-to-all-start
  97.4 4.6 %reduce = f32[4,65536]{1,0:T(4,128)S(1)} reduce(f32[4,1,65536]{2,1,0:T(1,128)} %all-to-all-done.1, f32[]{:T(128)} %broadcast.232), dimensions={1}, to_apply=%all_to_all.40.reduce_sub_computation | reduce | bytes 2097156 | tf_op jit(solution)/shard_map/all_to_all | solution.py:102
  102.0 5.6 %reshape.274 = f32[4096,1,2,32]{3,2,1,0:T(2,128)} reshape(f32[4,65536]{1,0:T(4,128)S(1)} %reduce) | data formatting | bytes 2097152
  107.6 5.3 %copy.86 = f32[1,2,32,4,1024]{4,3,2,1,0:T(4,128)S(1)} copy(f32[1,2,32,4,1024]{2,1,4,3,0:T(2,128)} %bitcast.151) | data formatting | bytes 2097152 | tf_op jit(solution)/shard_map/all_to_all | solution.py:102
  112.9 0.9 slice_bitcast_fusion.1
  113.8 10.5 %while.88 = (s32[]{:T(128)}, f32[32]{0:T(128)}, f32[32,1024]{1,0:T(8,128)S(1)}, f32[4,32]{1,0:T(4,128)S(1)}, f32[4,32,1024]{2,1,0:T(8,128)S(1)}, /*index=5*/f32[...) while((s32[]{:T(128)}, f32[32]{0:T(128)}, f32[32,1024]{1,0:T(8,128)S(1)}, ...), condition=%wide.region_2.3_spmd.clone, body=%wide.region_1.2_spmd.clone.sunk | while | flops 131139 | bytes 918649 | solution.py:107
  113.9 1.3 fusion.77
  115.2 1.2 constant_dynamic-slice_fusion.6
  116.5 1.3 fusion.77
  117.8 1.2 constant_dynamic-slice_fusion.6
  119.1 1.3 fusion.77
  120.4 1.2 constant_dynamic-slice_fusion.6
  121.7 1.3 fusion.77
  123.0 1.2 constant_dynamic-slice_fusion.6
  125.1 0.9 dynamic-update-slice
  126.1 6.0 %while.90 = (s32[]{:T(128)}, f32[32]{0:T(128)}, f32[32,1024]{1,0:T(8,128)S(1)}, f32[4,32]{1,0:T(4,128)S(1)}, f32[4,32,1024]{2,1,0:T(8,128)S(1)}, /*index=5*/f32[...) while((s32[]{:T(128)}, f32[32]{0:T(128)}, ...), condition=%wide.region_6.7_spmd.clone, body=%wide.region_5.6_spmd.clone.sunk | while | flops 131140 | bytes 918669 | solution.py:108
  126.1 1.2 fusion.80
  127.6 1.2 fusion.80
  129.1 1.2 fusion.80
  130.6 1.2 fusion.80
  132.9 17.3 %all-reduce.2 = (f32[256]{0:T(256)S(1)}, f32[256]{0:T(256)S(1)}) all-reduce(f32[256]{0:T(256)S(1)} %dynamic-update-slice.1, f32[256]{0:T(256)S(1)} %dynamic-update-slice), channel_id=4, replica_groups=mesh['outer'=8,'inner'=4] {'outer'}, use_global_device_ids=true, to_apply=%add.1 | all-reduce | flops 512 | bytes 4096
  150.4 13.0 %all-gather.7.cloned.1.call-done = f32[256,1024]{1,0:T(8,128)} async-done(((f32[32,1024]{1,0:T(8,128)}), f32[256,1024]{1,0:T(8,128)}) %all-gather.7.cloned.1.call-update) | async-done | bytes 1048592 | tf_op jit(solution)/shard_map/all_gather | solution.py:13
  163.3 8.2 %while.89 = (s32[]{:T(128)}, f32[32,1024]{1,0:T(8,128)S(1)}, s32[]{:T(128)}, f32[8,32]{1,0:T(8,128)S(1)}, f32[8,32,1024]{2,1,0:T(8,128)}, /*index=5*/s32[]{:T(128)}, s32[]{:T(128)}) while((s32[]{:T(128)}, f32[32,1024]{1,0:T(8,128)S(1)}, s32[]{:T(128)}, f32[8,32]{1,0:T(8,128)S(1)}, f32[8,32,1024]{2,1,0:T(8,128)}, ...), condition=%wide.region_4.5_spmd.clone, body=%wide.region_3.4_spmd.clone.sunk | while | flops 131076 | bytes 393705 | solution.py:26
  163.4 1.0 fusion.79
  164.4 1.0 fusion.79
  165.4 1.0 fusion.79
  166.5 1.0 fusion.79
  167.5 1.0 fusion.79
  168.5 1.0 fusion.79
  169.6 1.0 fusion.79
  170.6 1.0 fusion.79
  171.6 33.3 %all-gather.9.cloned.1.call-done = f32[256,1024]{1,0:T(8,128)} async-done(((f32[32,1024]{1,0:T(8,128)}), f32[256,1024]{1,0:T(8,128)}) %all-gather.9.cloned.1.call-update) | async-done | bytes 1048592 | tf_op jit(solution)/shard_map/all_gather | solution.py:13
  204.9 8.3 %while.91 = (s32[]{:T(128)}, f32[32,1024]{1,0:T(8,128)S(1)}, s32[]{:T(128)}, f32[8,32]{1,0:T(8,128)S(1)}, f32[8,32,1024]{2,1,0:T(8,128)}, /*index=5*/s32[]{:T(128)}, s32[]{:T(128)}, s32[]{:T(128)}, s32[]{:T(128)}) while((s32[]{:T(128)}, f32[32,1024]{1,0:T(8,128)S(1)}, s32[]{:T(128)}, f32[8,32]{1,0:T(8,128)S(1)}, ...), condition=%wide.region_8.9_spmd.clone, body=%wide.region_7.8_spmd.clone.sunk | while | flops 131080 | bytes 393767 | solution.py:26
  204.9 1.0 fusion.82
  205.9 1.0 fusion.82
  207.0 1.0 fusion.82
  208.0 1.0 fusion.82
  209.1 1.0 fusion.82
  210.1 1.0 fusion.82
  211.2 1.0 fusion.82
  212.2 1.0 fusion.82
  213.4 1.1 pad_maximum_fusion.1
  214.5 3.5 all-to-all-start.2
  218.3 1.0 bitcast_multiply_fusion.3
  219.7 3.5 fusion.15
  223.2 2.4 fusion.12
  225.7 6.7 %all-to-all-done.2 = f32[4,2,32,1024]{3,2,1,0:T(8,128)S(1)} async-done(((f32[4,2,32,1024]{3,2,1,0:T(8,128)}), f32[4,2,32,1024]{3,2,1,0:T(8,128)S(1)}, u32[]{:S(2)}, u32[]{:S(2)}) %all-to-all-start.2) | async-done | bytes 1048608 | tf_op jit(solution)/shard_map/all_to_all | solution.py:117
  233.0 2.2 fusion.18
  235.4 1.9 convolution_bitcast_fusion.1
  238.0 3.1 convolution_bitcast_fusion
  241.5 1.0 copy.87
  242.6 1.3 copy.80
  243.9 1.0 fusion.49
  244.9 131.4 %reduce-scatter.4.cloned.1.call-done = f32[32,128]{1,0:T(8,128)} async-done(((f32[1024,128]{1,0:T(8,128)}), f32[32,128]{1,0:T(8,128)}) %reduce-scatter.4.cloned.1.call-update) | async-done | bytes 16400
  (125 shorter events, 10.1 us)
Async XLA Ops:
  7.2 46.8 %copy-start = (bf16[128,1024]{1,0:T(8,128)(2,1)S(1)}, bf16[128,1024]{1,0:T(8,128)(2,1)}, u32[]{:S(2)}) copy-start(bf16[128,1024]{1,0:T(8,128)(2,1)} %param.14) | copy-start | bytes 786436
  7.2 47.1 %copy-start.8 = (f32[128,32]{0,1:T(8,128)S(1)}, f32[128,32]{0,1:T(8,128)}, u32[]{:S(2)}) copy-start(f32[128,32]{0,1:T(8,128)} %param.16) | copy-start | bytes 49156
  8.2 47.4 %copy-start.13 = (f32[32]{0:T(128)}, f32[32]{0:T(128)S(1)}, u32[]{:S(2)}) copy-start(f32[32]{0:T(128)S(1)} %slice_bitcast_fusion.2) | copy-start | bytes 388
  52.5 1.7 copy-start.3
  53.9 1.7 copy-start.5
  55.7 0.6 copy-start.6
  73.3 4.5 %copy-start.15 = (u32[32]{0:T(128)S(1)}, u32[32]{0:T(128)}, u32[]{:S(2)}) copy-start(u32[32]{0:T(128)} %constant.201) | copy-start | bytes 388
  73.3 18.9 %copy-start.14 = (f32[32]{0:T(128)S(1)}, f32[32]{0:T(128)}, u32[]{:S(2)}) copy-start(f32[32]{0:T(128)} %copy-done.13) | copy-start | bytes 388
  73.3 18.9 %all-to-all-start.1 = ((f32[4,1,65536]{2,1,0:T(1,128)}), f32[4,1,65536]{2,1,0:T(1,128)}, u32[]{:S(2)}, u32[]{:S(2)}) async-start(f32[4,1,65536]{2,1,0:T(1,128)} %reshape.273), calls=%async_computation.1 | async-start | bytes 2097152 | tf_op jit(solution)/shard_map/all_to_all | solution.py:102
  92.8 21.0 %all-to-all-start = ((f32[1,1,32,4]{2,1,0,3:T(1,128)}), f32[1,1,32,4]{2,1,0,3:T(1,128)}, u32[]{:S(2)}, u32[]{:S(2)}) async-start(f32[1,1,32,4]{2,1,0,3:T(1,128)} %broadcast_in_dim.120), calls=%async_computation | async-start | bytes 4096 | tf_op jit(solution)/shard_map/all_to_all | solution.py:103
  96.6 66.7 %all-gather.7.cloned.1.call-start = ((), (), s32[]{:S(2)}) async-start(), calls=%async_computation.4 | async-start | bytes 1179648 | tf_op jit(solution)/shard_map/all_gather | solution.py:13
  124.4 0.7 copy-start.2
  124.4 1.6 copy-start.11
  125.0 79.9 %all-gather.9.cloned.1.call-start = ((), (), s32[]{:S(2)}) async-start(), calls=%async_computation.5 | async-start | bytes 1179648 | tf_op jit(solution)/shard_map/all_gather | solution.py:13
  126.0 24.3 %copy-start.12 = (f32[4,32]{1,0:T(4,128)S(1)}, f32[4,32]{1,0:T(4,128)}, u32[]{:S(2)}) copy-start(f32[4,32]{1,0:T(4,128)} %copy-done.11) | copy-start | bytes 1540
  132.1 18.3 %copy-start.1 = (f32[32,1024]{1,0:T(8,128)}, f32[32,1024]{1,0:T(8,128)S(1)}, u32[]{:S(2)}) copy-start(f32[32,1024]{1,0:T(8,128)S(1)} %get-tuple-element.577) | copy-start | bytes 393220
  213.4 4.9 %copy-start.7 = (f32[128,32]{0,1:T(8,128)S(1)}, f32[128,32]{0,1:T(8,128)}, u32[]{:S(2)}) copy-start(f32[128,32]{0,1:T(8,128)} %copy-done.6) | copy-start | bytes 49156
  214.5 17.9 %all-to-all-start.2 = ((f32[4,2,32,1024]{3,2,1,0:T(8,128)}), f32[4,2,32,1024]{3,2,1,0:T(8,128)S(1)}, u32[]{:S(2)}, u32[]{:S(2)}) async-start(f32[4,2,32,1024]{3,2,1,0:T(8,128)} %pad_maximum_fusion.1), calls=%async_computation.2 | async-start | bytes 2097152 | tf_op jit(solution)/shard_map/all_to_all | solution.py:117
  218.0 158.3 %reduce-scatter.4.cloned.1.call-start = ((), (), s32[]{:S(2)}) async-start(), calls=%async_computation.6 | async-start | bytes 540672
  219.7 3.5 copy-start.9
  233.0 2.3 copy-start.10
  241.3 2.6 copy-start.4
Sparse Core Ops, SparseCore 0:
  125.2 38.1 all-gather.6
  166.0 38.8 all-gather.8
  242.7 133.5 reduce-scatter.3
where the time goes:
time: 384 us; the launch traced here: 383 us
  waiting for transfers between devices  198 us (52%)
  blocking collectives  61.5 us (16%)
  local copies, waits for them, and re-layouts  44.6 us (12%)
  other arithmetic  34 us (9%)
  matrix products  17.4 us (5%)
  between operations  14.8 us (4%)
  starting transfers between devices  12.3 us (3%)
    unnamed x4, waiting for transfers between devices  131 us
    all_gather x2, waiting for transfers between devices, carried_in(): everything = jax.tree.map(lambda part: lax.all_gather(part, axis), array)  46.3 us
    all_gather x1, blocking collectives, per_device(): weights_full = lax.all_gather(w_bc, ('outer', 'inner'), axis=0, tiled=True)  44.2 us
    unnamed x45, local copies, waits for them, and re-layouts  25 us
    unnamed x1, blocking collectives  17.3 us
    select_n x16, other arithmetic, step(): return jax.tree.map(lambda a, b: jnp.where(reached, a, b), new, before)  15.9 us
    all_to_all x1, waiting for transfers between devices, per_device(): lax.all_to_all(paired, 'inner', split_axis=3, concat_axis=0, tiled=True)  13.3 us
    exp x8, other arithmetic, slice_combine(): jnp.exp(later[0])[:, None] * earlier[1] + later[1]  9.94 us
  transfers between devices with their start and end apart: 6, of which 5 were waited for; matrix products, arithmetic and copies ran while one was open for 11% of the time, Pallas kernels for 0%

commit v1 on v0

--- a/solution.py
+++ b/solution.py
@@ -99,7 +99,12 @@
     )[None]
     totals_wide = jnp.broadcast_to(totals[None, None, :, None], (1, 1, head_count, inner_count))
     slices, all_totals = (
-        lax.all_to_all(paired, "inner", split_axis=3, concat_axis=0, tiled=True),
+        jnp.concatenate(
+            lax.all_to_all(
+                jnp.stack(jnp.split(paired, lax.axis_size("inner"), axis=3)), "inner", 0, 0
+            ),
+            axis=0,
+        ),
         lax.all_to_all(totals_wide, "inner", split_axis=3, concat_axis=0, tiled=True),
     )
     all_totals = all_totals[:, 0, :, 0]

time: 384 us -> 353 us (0.919)
  local copies, waits for them, and re-layouts: 44.6 us -> 13.4 us
    unnamed x45 -> x46, local copies, waits for them, and re-layouts: 25 us -> 8.31 us
    all_to_all x2 -> x0, local copies, waits for them, and re-layouts: 5.84 us -> none  [per_device(): lax.all_to_all(paired, 'inner', split_axis=3, concat_axis=0, tiled=True)]
    dynamic_slice x8 -> x0, local copies, waits for them, and re-layouts: 5.31 us -> none  [per_device(): lax.scan(slice_step, zero_slice, (all_totals, slices[:, 0]))]
    all_to_all x1 -> x0, other arithmetic: 4.61 us -> none  [per_device(): lax.all_to_all(paired, 'inner', split_axis=3, concat_axis=0, tiled=True)]
    another operation x3 -> x2, local copies, waits for them, and re-layouts: 5.13 us -> 0.72 us  [per_device(): jnp.stack([own_state.reshape(head_count, flat_width), own_adjoint.reshape...]
  transfers between devices with their start and end apart: 6 -> 6, of which waited for: 5 -> 6; matrix products, arithmetic and copies ran while one was open for 11% -> 8% of each run, Pallas kernels for 0% -> 0%
where the time goes in v1:
time: 353 us; the launch traced here: 352 us
  waiting for transfers between devices  199 us (56%)
  blocking collectives  61.4 us (17%)
  other arithmetic  33.9 us (10%)
  matrix products  17.4 us (5%)
  between operations  14.9 us (4%)
  local copies, waits for them, and re-layouts  13.4 us (4%)
  starting transfers between devices  11.4 us (3%)
    unnamed x4, waiting for transfers between devices  131 us
    all_gather x2, waiting for transfers between devices, carried_in(): everything = jax.tree.map(lambda part: lax.all_gather(part, axis), array)  45.1 us
    all_gather x1, blocking collectives, per_device(): weights_full = lax.all_gather(w_bc, ('outer', 'inner'), axis=0, tiled=True)  44.2 us
    unnamed x1, blocking collectives  17.2 us
    select_n x16, other arithmetic, step(): return jax.tree.map(lambda a, b: jnp.where(reached, a, b), new, before)  15.9 us
    all_to_all x1, waiting for transfers between devices, per_device(): lax.all_to_all(jnp.stack(jnp.split(paired, lax.axis_size('inner'), axis=3...  13.1 us
    exp x8, other arithmetic, slice_combine(): jnp.exp(later[0])[:, None] * earlier[1] + later[1]  9.85 us
    unnamed x46, local copies, waits for them, and re-layouts  8.31 us
  transfers between devices with their start and end apart: 6, of which 6 were waited for; matrix products, arithmetic and copies ran while one was open for 8% of the time, Pallas kernels for 0%

profile of v1, /device:TPU:0, one launch (start us, length us, event | category | flops | bytes accessed | tf_op | source)
XLA Modules:
  0.0 352.2 jit_solution(10642059735456077125)
XLA Ops:
  7.2 0.9 copy.47
  8.8 44.2 %all_gather.27 = bf16[1024,128]{1,0:T(8,128)(2,1)S(1)} all-gather(bf16[32,128]{1,0:T(8,128)(2,1)} %param.18), channel_id=1, replica_groups=mesh['outer'=8,'inner'=4] {'outer','inner'}, dimensions={0}, use_global_device_ids=true | all-gather | bytes 270336 | tf_op jit(solution)/shard_map/all_gather | solution.py:72
  53.7 1.0 fusion.27
  55.1 0.6 copy-done.7
  56.4 1.0 fusion.25
  57.9 1.0 pad_maximum_fusion
  58.9 3.6 %all-to-all-start.1 = ((f32[4,1,2,32,1024]{4,3,2,1,0:T(8,128)}), f32[4,1,2,32,1024]{4,3,2,1,0:T(8,128)S(1)}, u32[]{:S(2)}, u32[]{:S(2)}) async-start(f32[4,1,2,32,1024]{4,3,2,1,0:T(8,128)} %pad_maximum_fusion), calls=%async_computation.1 | async-start | bytes 2097152 | tf_op jit(solution)/shard_map/all_to_all | solution.py:103
  62.6 0.6 dynamic-slice.3
  63.9 13.1 %all-to-all-done.1 = f32[4,1,2,32,1024]{4,3,2,1,0:T(8,128)S(1)} async-done(((f32[4,1,2,32,1024]{4,3,2,1,0:T(8,128)}), f32[4,1,2,32,1024]{4,3,2,1,0:T(8,128)S(1)}, u32[]{:S(2)}, u32[]{:S(2)}) %all-to-all-start.1) | async-done | bytes 1048608 | tf_op jit(solution)/shard_map/all_to_all | solution.py:103
  77.5 3.8 %all-to-all-start = ((f32[1,1,32,4]{2,1,0,3:T(1,128)}), f32[1,1,32,4]{2,1,0,3:T(1,128)}, u32[]{:S(2)}, u32[]{:S(2)}) async-start(f32[1,1,32,4]{2,1,0,3:T(1,128)} %broadcast_in_dim.120), calls=%async_computation | async-start | bytes 4096 | tf_op jit(solution)/shard_map/all_to_all | solution.py:108
  81.4 0.9 slice_bitcast_fusion.1
  82.3 2.8 all-to-all-done
  85.2 9.3 %while.88 = (s32[]{:T(128)}, f32[32]{0:T(128)}, f32[32,1024]{1,0:T(8,128)S(1)}, f32[4,32]{1,0:T(4,128)S(1)}, f32[4,32,1024]{2,1,0:T(8,128)S(1)}, /*index=5*/f32[...) while((s32[]{:T(128)}, f32[32]{0:T(128)}, f32[32,1024]{1,0:T(8,128)S(1)}, ...), condition=%wide.region_2.3_spmd.clone, body=%wide.region_1.2_spmd.clone.sunk | while | flops 131139 | bytes 656505 | solution.py:112
  85.2 1.3 fusion.73
  86.5 1.0 bitcast_add_fusion.6
  87.5 1.3 fusion.73
  88.8 1.0 bitcast_add_fusion.6
  89.8 1.3 fusion.73
  91.1 1.0 bitcast_add_fusion.6
  92.1 1.3 fusion.73
  93.4 1.0 bitcast_add_fusion.6
  94.5 0.6 copy-done.2
  95.2 0.9 dynamic-update-slice
  96.1 5.4 %while.90 = (s32[]{:T(128)}, f32[32]{0:T(128)}, f32[32,1024]{1,0:T(8,128)S(1)}, f32[4,32]{1,0:T(4,128)S(1)}, f32[4,32,1024]{2,1,0:T(8,128)S(1)}, /*index=5*/f32[...) while((s32[]{:T(128)}, f32[32]{0:T(128)}, ...), condition=%wide.region_6.7_spmd.clone, body=%wide.region_5.6_spmd.clone.sunk | while | flops 131140 | bytes 656525 | solution.py:113
  96.1 1.2 fusion.75
  97.5 1.2 fusion.75
  98.9 1.2 fusion.75
  100.2 1.2 fusion.75
  101.6 0.8 dynamic-update-slice.1
  102.4 17.2 %all-reduce.2 = (f32[256]{0:T(256)S(1)}, f32[256]{0:T(256)S(1)}) all-reduce(f32[256]{0:T(256)S(1)} %dynamic-update-slice.1, f32[256]{0:T(256)S(1)} %dynamic-update-slice), channel_id=4, replica_groups=mesh['outer'=8,'inner'=4] {'outer'}, use_global_device_ids=true, to_apply=%add.1 | all-reduce | flops 512 | bytes 4096
  119.9 11.6 %all-gather.7.cloned.1.call-done = f32[256,1024]{1,0:T(8,128)} async-done(((f32[32,1024]{1,0:T(8,128)}), f32[256,1024]{1,0:T(8,128)}) %all-gather.7.cloned.1.call-update) | async-done | bytes 1048592 | tf_op jit(solution)/shard_map/all_gather | solution.py:13
  131.5 8.2 %while.89 = (s32[]{:T(128)}, f32[32,1024]{1,0:T(8,128)S(1)}, s32[]{:T(128)}, f32[8,32]{1,0:T(8,128)S(1)}, f32[8,32,1024]{2,1,0:T(8,128)}, /*index=5*/s32[]{:T(128)}, s32[]{:T(128)}) while((s32[]{:T(128)}, f32[32,1024]{1,0:T(8,128)S(1)}, s32[]{:T(128)}, f32[8,32]{1,0:T(8,128)S(1)}, f32[8,32,1024]{2,1,0:T(8,128)}, ...), condition=%wide.region_4.5_spmd.clone, body=%wide.region_3.4_spmd.clone.sunk | while | flops 131076 | bytes 393705 | solution.py:26
  131.5 1.0 fusion.74
  132.5 1.0 fusion.74
  133.6 1.0 fusion.74
  134.6 1.0 fusion.74
  135.6 1.0 fusion.74
  136.7 1.0 fusion.74
  137.7 1.0 fusion.74
  138.7 1.0 fusion.74
  139.7 33.5 %all-gather.9.cloned.1.call-done = f32[256,1024]{1,0:T(8,128)} async-done(((f32[32,1024]{1,0:T(8,128)}), f32[256,1024]{1,0:T(8,128)}) %all-gather.9.cloned.1.call-update) | async-done | bytes 1048592 | tf_op jit(solution)/shard_map/all_gather | solution.py:13
  173.2 8.3 %while.91 = (s32[]{:T(128)}, f32[32,1024]{1,0:T(8,128)S(1)}, s32[]{:T(128)}, f32[8,32]{1,0:T(8,128)S(1)}, f32[8,32,1024]{2,1,0:T(8,128)}, /*index=5*/s32[]{:T(128)}, s32[]{:T(128)}, s32[]{:T(128)}, s32[]{:T(128)}) while((s32[]{:T(128)}, f32[32,1024]{1,0:T(8,128)S(1)}, s32[]{:T(128)}, f32[8,32]{1,0:T(8,128)S(1)}, ...), condition=%wide.region_8.9_spmd.clone, body=%wide.region_7.8_spmd.clone.sunk | while | flops 131080 | bytes 393767 | solution.py:26
  173.2 1.0 fusion.76
  174.3 1.0 fusion.76
  175.3 1.0 fusion.76
  176.4 1.0 fusion.76
  177.4 1.0 fusion.76
  178.5 1.0 fusion.76
  179.5 1.0 fusion.76
  180.5 1.0 fusion.76
  181.7 1.1 pad_maximum_fusion.1
  182.8 3.6 %all-to-all-start.2 = ((f32[4,2,32,1024]{3,2,1,0:T(8,128)}), f32[4,2,32,1024]{3,2,1,0:T(8,128)S(1)}, u32[]{:S(2)}, u32[]{:S(2)}) async-start(f32[4,2,32,1024]{3,2,1,0:T(8,128)} %pad_maximum_fusion.1), calls=%async_computation.2 | async-start | bytes 2097152 | tf_op jit(solution)/shard_map/all_to_all | solution.py:122
  186.7 1.0 bitcast_multiply_fusion.3
  188.1 3.5 fusion.13
  191.6 2.4 fusion.10
  194.1 6.8 %all-to-all-done.2 = f32[4,2,32,1024]{3,2,1,0:T(8,128)S(1)} async-done(((f32[4,2,32,1024]{3,2,1,0:T(8,128)}), f32[4,2,32,1024]{3,2,1,0:T(8,128)S(1)}, u32[]{:S(2)}, u32[]{:S(2)}) %all-to-all-start.2) | async-done | bytes 1048608 | tf_op jit(solution)/shard_map/all_to_all | solution.py:122
  201.4 2.2 fusion.16
  203.9 1.9 convolution_bitcast_fusion.1
  205.8 1.4 squeeze.114
  207.4 3.1 convolution_bitcast_fusion
  211.0 1.0 copy.66
  212.0 1.3 copy.60
  213.3 1.0 fusion.47
  214.3 131.4 %reduce-scatter.4.cloned.1.call-done = f32[32,128]{1,0:T(8,128)} async-done(((f32[1024,128]{1,0:T(8,128)}), f32[32,128]{1,0:T(8,128)}) %reduce-scatter.4.cloned.1.call-update) | async-done | bytes 16400
  (116 shorter events, 7.0 us)
Async XLA Ops:
  7.2 46.1 %copy-start = (bf16[128,1024]{1,0:T(8,128)(2,1)S(1)}, bf16[128,1024]{1,0:T(8,128)(2,1)}, u32[]{:S(2)}) copy-start(bf16[128,1024]{1,0:T(8,128)(2,1)} %param.14) | copy-start | bytes 786436
  7.2 45.8 %copy-start.6 = (bf16[128,2048]{1,0:T(8,128)(2,1)S(1)}, bf16[128,2048]{1,0:T(8,128)(2,1)}, u32[]{:S(2)}) copy-start(bf16[128,2048]{1,0:T(8,128)(2,1)} %param.15) | copy-start | bytes 1572868
  8.3 0.5 copy-start.15
  8.3 45.5 %copy-start.10 = (f32[128,32]{0,1:T(8,128)S(1)}, f32[128,32]{0,1:T(8,128)}, u32[]{:S(2)}) copy-start(f32[128,32]{0,1:T(8,128)} %param.16) | copy-start | bytes 49156
  53.0 0.7 copy-start.4
  54.7 1.0 copy-start.7
  55.8 0.6 copy-start.8
  58.9 3.7 %copy-start.17 = (u32[32]{0:T(128)S(1)}, u32[32]{0:T(128)}, u32[]{:S(2)}) copy-start(u32[32]{0:T(128)} %constant.201) | copy-start | bytes 388
  58.9 18.1 %copy-start.16 = (f32[32]{0:T(128)S(1)}, f32[32]{0:T(128)}, u32[]{:S(2)}) copy-start(f32[32]{0:T(128)} %copy-done.15) | copy-start | bytes 388
  58.9 18.1 %all-to-all-start.1 = ((f32[4,1,2,32,1024]{4,3,2,1,0:T(8,128)}), f32[4,1,2,32,1024]{4,3,2,1,0:T(8,128)S(1)}, u32[]{:S(2)}, u32[]{:S(2)}) async-start(f32[4,1,2,32,1024]{4,3,2,1,0:T(8,128)} %pad_maximum_fusion), calls=%async_computation.1 | async-start | bytes 2097152 | tf_op jit(solution)/shard_map/all_to_all | solution.py:103
  77.5 7.6 %all-to-all-start = ((f32[1,1,32,4]{2,1,0,3:T(1,128)}), f32[1,1,32,4]{2,1,0,3:T(1,128)}, u32[]{:S(2)}, u32[]{:S(2)}) async-start(f32[1,1,32,4]{2,1,0,3:T(1,128)} %broadcast_in_dim.120), calls=%async_computation | async-start | bytes 4096 | tf_op jit(solution)/shard_map/all_to_all | solution.py:108
  81.4 50.1 %all-gather.7.cloned.1.call-start = ((), (), s32[]{:S(2)}) async-start(), calls=%async_computation.4 | async-start | bytes 1179648 | tf_op jit(solution)/shard_map/all_gather | solution.py:13
  94.4 0.7 copy-start.2
  94.5 1.6 copy-start.13
  95.1 78.1 %all-gather.9.cloned.1.call-start = ((), (), s32[]{:S(2)}) async-start(), calls=%async_computation.5 | async-start | bytes 1179648 | tf_op jit(solution)/shard_map/all_gather | solution.py:13
  96.1 23.7 %copy-start.14 = (f32[4,32]{1,0:T(4,128)S(1)}, f32[4,32]{1,0:T(4,128)}, u32[]{:S(2)}) copy-start(f32[4,32]{1,0:T(4,128)} %copy-done.13) | copy-start | bytes 1540
  101.6 18.3 %copy-start.1 = (f32[32,1024]{1,0:T(8,128)}, f32[32,1024]{1,0:T(8,128)S(1)}, u32[]{:S(2)}) copy-start(f32[32,1024]{1,0:T(8,128)S(1)} %get-tuple-element.577) | copy-start | bytes 393220
  182.8 3.9 %copy-start.9 = (f32[128,32]{0,1:T(8,128)S(1)}, f32[128,32]{0,1:T(8,128)}, u32[]{:S(2)}) copy-start(f32[128,32]{0,1:T(8,128)} %copy-done.8) | copy-start | bytes 49156
  182.8 18.1 %all-to-all-start.2 = ((f32[4,2,32,1024]{3,2,1,0:T(8,128)}), f32[4,2,32,1024]{3,2,1,0:T(8,128)S(1)}, u32[]{:S(2)}, u32[]{:S(2)}) async-start(f32[4,2,32,1024]{3,2,1,0:T(8,128)} %pad_maximum_fusion.1), calls=%async_computation.2 | async-start | bytes 2097152 | tf_op jit(solution)/shard_map/all_to_all | solution.py:122
  186.4 159.3 %reduce-scatter.4.cloned.1.call-start = ((), (), s32[]{:S(2)}) async-start(), calls=%async_computation.6 | async-start | bytes 540672
  188.1 3.5 %copy-start.11 = (f32[128,32]{0,1:T(8,128)S(1)}, f32[128,32]{0,1:T(8,128)}, u32[]{:S(2)}) copy-start(f32[128,32]{0,1:T(8,128)} %param.16) | copy-start | bytes 49156
  201.4 2.3 copy-start.12
  205.8 1.7 copy-start.3
  212.0 1.3 copy-start.5
Sparse Core Ops, SparseCore 0:
  95.2 36.2 all-gather.6
  134.2 38.9 all-gather.8
  212.1 133.5 reduce-scatter.3
